TPU v7x, 256 devices: a whole 4x4x8 slice. The times are simulated.
256 devices in a mesh: section: 16 (over x, y_lo, core), dp: 16 (over y_hi, z).
Axes of the slice: x: 4, y: 4 (y_hi: 2, y_lo: 2; y = y_hi * 2 + y_lo), z: 8, core: 2. Of those that a mesh axis runs over, the one named last changes fastest.
Arguments:
- inputs: bfloat16 [16, 2, 4096, 2048], P('section', None, 'dp'), may hold values from -6 to 6
- cotangent: bfloat16 [16, 2, 4096, 2048], P('section', None, 'dp'), may hold values from -6 to 6
- w_gate: bfloat16 [16, 2, 2048, 256], P('section'), may hold values from -0.125 to 0.125
- w_up: bfloat16 [16, 2, 2048, 256], P('section'), may hold values from -0.125 to 0.125
- w_down: bfloat16 [16, 2, 256, 2048], P('section'), may hold values from -0.375 to 0.375
- mom_gate: float32 [16, 2048, 256], P('section', 'dp'), may hold values from -6 to 6
- mom_up: float32 [16, 2048, 256], P('section', 'dp'), may hold values from -6 to 6
- mom_down: float32 [16, 2048, 256], P('section', 'dp'), may hold values from -6 to 6
Outputs:
- grad_in: bfloat16 [16, 2, 4096, 2048], P('section', None, 'dp')
- new_gate: float32 [16, 2048, 256], P('section', 'dp')
- new_up: float32 [16, 2048, 256], P('section', 'dp')
- new_down: float32 [16, 2048, 256], P('section', 'dp')
All inputs are finite; a program needn't handle non-finite values.
Results may differ from a plain program's by a relative error of at most 0.009.
Values may be sent and summed in bfloat16 or wider, within the bound.
A program may use at most 128 MiB of HBM per device.

v0:
```python
import jax
import jax.numpy as jnp
from jax import lax
from jax.sharding import PartitionSpec as P


def from_behind(value, axis, steps):
    count = lax.axis_size(axis)
    first, last = (max(0, -steps), min(count, count - steps))
    return lax.ppermute(value, axis, [(source, source + steps) for source in range(first, last)])


def from_partner(value, axis, stride):
    mask = 2**stride
    pairs = [(source, source ^ mask) for source in range(lax.axis_size(axis))]
    return lax.ppermute(value, axis, pairs)


def contract_rows(left, right):
    return lax.dot_general(
        left, right, (((0,), (0,)), ((), ())), preferred_element_type=jnp.float32
    )


def backward_block(block_in, block_cot, gate_mat, up_mat, down_mat):
    gate_pre = jnp.dot(block_in, gate_mat, preferred_element_type=jnp.float32)
    up_pre = jnp.dot(block_in, up_mat, preferred_element_type=jnp.float32)
    sigmoid_val = jax.nn.sigmoid(gate_pre)
    activated = gate_pre * sigmoid_val
    hidden = (activated * up_pre).astype(jnp.bfloat16)
    hidden_grad = lax.dot_general(
        block_cot, down_mat, (((1,), (1,)), ((), ())), preferred_element_type=jnp.float32
    )
    gate_grad = (
        hidden_grad * up_pre * sigmoid_val * (1.0 + gate_pre * (1.0 - sigmoid_val))
    ).astype(jnp.bfloat16)
    up_grad = (hidden_grad * activated).astype(jnp.bfloat16)
    input_grad = (
        lax.dot_general(
            gate_grad, gate_mat, (((1,), (1,)), ((), ())), preferred_element_type=jnp.float32
        )
        + lax.dot_general(
            up_grad, up_mat, (((1,), (1,)), ((), ())), preferred_element_type=jnp.float32
        )
    ).astype(jnp.bfloat16)
    grad_gate_w = contract_rows(block_in, gate_grad)
    grad_up_w = contract_rows(block_in, up_grad)
    grad_down_w = contract_rows(block_cot, hidden)
    return (input_grad, grad_gate_w, grad_up_w, grad_down_w)


def body(inputs, cotangent, w_gate, w_up, w_down, mom_gate, mom_up, mom_down):
    first = backward_block(inputs[0, 0], cotangent[0, 0], w_gate[0, 0], w_up[0, 0], w_down[0, 0])
    second = backward_block(inputs[0, 1], cotangent[0, 1], w_gate[0, 1], w_up[0, 1], w_down[0, 1])
    recv_first = from_behind(first[0], "section", -1)
    recv_second = from_behind(second[0], "section", 1)
    grad_in = jnp.stack([recv_first, recv_second])[None]
    second_rounded = jnp.stack([second[1], second[2], second[3]]).astype(jnp.bfloat16)
    bit_count = lax.axis_size("section").bit_length() - 1
    mirrored = second_rounded
    for bit_index in range(bit_count):
        mirrored = from_partner(mirrored, "section", bit_index)
    mirrored = mirrored.astype(jnp.float32)
    summed_gate, summed_up, summed_down = (
        lax.psum_scatter(first[1] + mirrored[0], "dp", scatter_dimension=0, tiled=True),
        lax.psum_scatter(first[2] + mirrored[1], "dp", scatter_dimension=0, tiled=True),
        lax.psum_scatter(first[3] + mirrored[2], "dp", scatter_dimension=0, tiled=True),
    )
    total_rows = inputs.shape[2] * lax.axis_size("dp")
    scale_factor = 1.0 / jnp.sqrt(jnp.float32(total_rows))
    new_gate = 0.9 * mom_gate[0] + summed_gate * scale_factor
    new_up = 0.9 * mom_up[0] + summed_up * scale_factor
    new_down = 0.9 * mom_down[0] + summed_down * scale_factor
    return (grad_in, new_gate[None], new_up[None], new_down[None])


def solution(mesh):
    placed = (
        P("section", None, "dp", None),
        P("section", None, "dp", None),
        P("section", None, None, None),
        P("section", None, None, None),
        P("section", None, None, None),
        P("section", "dp", None),
        P("section", "dp", None),
        P("section", "dp", None),
    )
    return jax.shard_map(
        body,
        mesh=mesh,
        in_specs=placed,
        out_specs=(
            P("section", None, "dp", None),
            P("section", "dp", None),
            P("section", "dp", None),
            P("section", "dp", None),
        ),
        check_vma=False,
    )
```

profile of v0, /device:TPU:1, one launch (start us, length us, event | category | flops | bytes accessed | tf_op | source)
XLA Modules:
  0.0 874.8 jit_solution(16092099013627418138)
XLA Ops:
  7.2 2.1 fusion.10
  9.4 1.8 fusion.13
  11.8 1.1 copy-done.9
  14.7 3.3 collective-permute-start.2
  18.0 5.3 collective-permute-done.2
  23.2 69.3 %collective-permute-done.3 = bf16[3,2048,256]{1,2,0:T(8,128)(2,1)S(1)} collective-permute-done((bf16[3,2048,256]{1,2,0:T(8,128)(2,1)S(1)}, bf16[3,2048,256]{1,2,0:T(8,128)(2,1)S(1)}, u32[]{:S(2)}, u32[]{:S(2)}) %collective-permute-start.3) | collective-permute-done | bytes 3145760 | tf_op jit(solution)/shard_map/ppermute | solution.py:16
  92.5 68.4 %collective-permute-done.4 = bf16[3,2048,256]{1,2,0:T(8,128)(2,1)S(1)} collective-permute-done((bf16[3,2048,256]{1,2,0:T(8,128)(2,1)S(1)}, bf16[3,2048,256]{1,2,0:T(8,128)(2,1)S(1)}, u32[]{:S(2)}, u32[]{:S(2)}) %collective-permute-start.4) | collective-permute-done | bytes 3145760 | tf_op jit(solution)/shard_map/ppermute | solution.py:16
  161.0 1.0 collective-permute-start.5
  163.4 66.7 %collective-permute-done.5 = bf16[3,2048,256]{1,2,0:T(8,128)(2,1)S(1)} collective-permute-done((bf16[3,2048,256]{1,2,0:T(8,128)(2,1)S(1)}, bf16[3,2048,256]{1,2,0:T(8,128)(2,1)S(1)}, u32[]{:S(2)}, u32[]{:S(2)}) %collective-permute-start.5) | collective-permute-done | bytes 3145760 | tf_op jit(solution)/shard_map/ppermute | solution.py:16
  230.0 0.8 convert_element_type.35
  230.9 2.7 copy-done
  233.6 1.8 fusion.7
  235.4 3.4 fusion.6
  239.0 1.5 copy-done.7
  240.5 3.4 fusion.5
  243.9 1.6 copy-done.3
  246.0 1.1 copy-done.5
  247.1 1.5 fusion
  248.5 4.8 collective-permute-start
  254.4 2.4 collective-permute-start.1
  256.8 1.0 copy.13
  257.8 1.0 copy.14
  258.9 7.7 collective-permute-done
  266.5 10.9 %collective-permute-done.1 = bf16[256,2048]{1,0:T(8,128)(2,1)S(1)} collective-permute-done((bf16[256,2048]{1,0:T(8,128)(2,1)S(1)}, bf16[256,2048]{1,0:T(8,128)(2,1)S(1)}, u32[]{:S(2)}, u32[]{:S(2)}) %collective-permute-start.1) | collective-permute-done | bytes 1048608 | tf_op jit(solution)/shard_map/ppermute | solution.py:10
  277.4 1.5 maximum_bitcast_fusion
  278.9 164.6 %reduce-scatter.4.cloned.1.call-done = f32[128,256]{0,1:T(8,128)} async-done(((f32[2048,256]{0,1:T(8,128)}), f32[128,256]{0,1:T(8,128)}) %reduce-scatter.4.cloned.1.call-update) | async-done | bytes 131088 | tf_op jit(solution)/shard_map/reduce_scatter | solution.py:65
  443.6 0.9 fusion.70
  444.5 0.8 copy.15
  445.3 209.8 %reduce-scatter.6.cloned.1.call-done = f32[128,256]{0,1:T(8,128)} async-done(((f32[2048,256]{0,1:T(8,128)}), f32[128,256]{0,1:T(8,128)}) %reduce-scatter.6.cloned.1.call-update) | async-done | bytes 131088 | tf_op jit(solution)/shard_map/reduce_scatter | solution.py:66
  655.0 0.9 fusion.69
  656.7 209.9 %reduce-scatter.8.cloned.1.call-done = f32[128,256]{0,1:T(8,128)} async-done(((f32[2048,256]{0,1:T(8,128)}), f32[128,256]{0,1:T(8,128)}) %reduce-scatter.8.cloned.1.call-update) | async-done | bytes 131088 | tf_op jit(solution)/shard_map/reduce_scatter | solution.py:67
  866.6 0.9 fusion.68
  (37 shorter events, 6.9 us)
Async XLA Ops:
  7.2 2.2 copy-start.1
  7.2 436.4 %reduce-scatter.4.cloned.1.call-start = ((), (), s32[]{:S(2)}) async-start(), calls=%async_computation.3 | async-start | bytes 2228224 | tf_op jit(solution)/shard_map/reduce_scatter | solution.py:65
  9.4 1.9 copy-start.6
  11.3 1.6 copy-start.9
  14.3 147.7 %copy-start.2 = (bf16[1,2,2048,256]{3,2,1,0:T(8,128)(2,1)S(1)}, bf16[1,2,2048,256]{3,2,1,0:T(8,128)(2,1)}, u32[]{:S(2)}) copy-start(bf16[1,2,2048,256]{3,2,1,0:T(8,128)(2,1)} %param.10) | copy-start | bytes 6291460
  14.7 147.8 %copy-start.4 = (bf16[1,2,2048,256]{3,2,1,0:T(8,128)(2,1)S(1)}, bf16[1,2,2048,256]{3,2,1,0:T(8,128)(2,1)}, u32[]{:S(2)}) copy-start(bf16[1,2,2048,256]{3,2,1,0:T(8,128)(2,1)} %param.11) | copy-start | bytes 6291460
  14.7 8.6 collective-permute-start.2
  23.2 69.3 %collective-permute-start.3 = (bf16[3,2048,256]{1,2,0:T(8,128)(2,1)S(1)}, bf16[3,2048,256]{1,2,0:T(8,128)(2,1)S(1)}, u32[]{:S(2)}, u32[]{:S(2)}) collective-permute-start(bf16[3,2048,256]{1,2,0:T(8,128)(2,1)S(1)} %collective-permute-done.2), channel_id=1, source_target_pairs={{0,32},{16,48},{32,0},{48,16},{64,96},{80,112},{96,64},{112,80},{1... | collective-permute-start | bytes 9437192 | tf_op jit(solution)/shard_map/ppermute | solution.py:16
  92.5 68.4 %collective-permute-start.4 = (bf16[3,2048,256]{1,2,0:T(8,128)(2,1)S(1)}, bf16[3,2048,256]{1,2,0:T(8,128)(2,1)S(1)}, u32[]{:S(2)}, u32[]{:S(2)}) collective-permute-start(bf16[3,2048,256]{1,2,0:T(8,128)(2,1)S(1)} %collective-permute-done.3), channel_id=1, source_target_pairs={{0,64},{16,80},{32,96},{48,112},{64,0},{80,16},{96,32},{112,48},{1... | collective-permute-start | bytes 9437192 | tf_op jit(solution)/shard_map/ppermute | solution.py:16
  161.0 69.1 %collective-permute-start.5 = (bf16[3,2048,256]{1,2,0:T(8,128)(2,1)S(1)}, bf16[3,2048,256]{1,2,0:T(8,128)(2,1)S(1)}, u32[]{:S(2)}, u32[]{:S(2)}) collective-permute-start(bf16[3,2048,256]{1,2,0:T(8,128)(2,1)S(1)} %collective-permute-done.4), channel_id=1, source_target_pairs={{0,128},{16,144},{32,160},{48,176},{64,192},{80,208},{96,224},{112... | collective-permute-start | bytes 9437192 | tf_op jit(solution)/shard_map/ppermute | solution.py:16
  230.9 2.7 copy-start
  235.4 419.6 %reduce-scatter.6.cloned.1.call-start = ((), (), s32[]{:S(2)}) async-start(), calls=%async_computation.4 | async-start | bytes 2228224 | tf_op jit(solution)/shard_map/reduce_scatter | solution.py:66
  238.9 1.6 copy-start.7
  238.9 627.7 %reduce-scatter.8.cloned.1.call-start = ((), (), s32[]{:S(2)}) async-start(), calls=%async_computation.5 | async-start | bytes 2228224 | tf_op jit(solution)/shard_map/reduce_scatter | solution.py:67
  243.9 1.6 copy-start.3
  245.5 1.6 copy-start.5
  248.5 18.0 %collective-permute-start = (bf16[256,2048]{1,0:T(8,128)(2,1)}, bf16[256,2048]{1,0:T(8,128)(2,1)S(1)}, u32[]{:S(2)}, u32[]{:S(2)}) collective-permute-start(bf16[256,2048]{1,0:T(8,128)(2,1)} %fusion), channel_id=1, source_target_pairs={{16,0},{32,16},{48,32},{64,48},{80,64},{96,80},{112,96},{128,112},... | collective-permute-start | bytes 3145736 | tf_op jit(solution)/shard_map/ppermute | solution.py:10
  253.9 2.9 copy-start.8
  254.4 23.1 %collective-permute-start.1 = (bf16[256,2048]{1,0:T(8,128)(2,1)S(1)}, bf16[256,2048]{1,0:T(8,128)(2,1)S(1)}, u32[]{:S(2)}, u32[]{:S(2)}) collective-permute-start(bf16[256,2048]{1,0:T(8,128)(2,1)S(1)} %fusion.1), channel_id=1, source_target_pairs={{0,16},{16,32},{32,48},{48,64},{64,80},{80,96},{96,112},{112,128},... | collective-permute-start | bytes 3145736 | tf_op jit(solution)/shard_map/ppermute | solution.py:10
Sparse Core Ops, SparseCore 0:
  235.5 208.0 reduce-scatter.3
  447.5 207.5 reduce-scatter.5
  658.9 207.5 reduce-scatter.7
where the time goes:
time: 880 us; the launch traced here: 875 us
  waiting for transfers between devices  813 us (92%)
  matrix products  18.7 us (2%)
  between operations  14 us (2%)
  local copies, waits for them, and re-layouts  12.5 us (1%)
  starting transfers between devices  11.7 us (1%)
    reduce_scatter x1, waiting for transfers between devices, body(): lax.psum_scatter(first[3] + mirrored[2], 'dp', scatter_dimension=0, tiled...  210 us
    reduce_scatter x1, waiting for transfers between devices, body(): lax.psum_scatter(first[2] + mirrored[1], 'dp', scatter_dimension=0, tiled...  210 us
    ppermute x4, waiting for transfers between devices, from_partner(): return lax.ppermute(value, axis, pairs)  210 us
    reduce_scatter x1, waiting for transfers between devices, body(): lax.psum_scatter(first[1] + mirrored[0], 'dp', scatter_dimension=0, tiled...  165 us
    ppermute x2, waiting for transfers between devices, from_behind(): lax.ppermute(value, axis, [(source, source + steps) for source in range(f...  18.6 us
  transfers between devices with their start and end apart: 9, of which 9 were waited for; matrix products, arithmetic and copies ran while one was open for 2% of the time, Pallas kernels for 0%

commit v1 on v0

v1 whole, which is shorter than its diff:
```python
import functools

import jax
import jax.numpy as jnp
from jax import lax
from jax.experimental import pallas as pl
from jax.experimental.pallas import tpu as pltpu
from jax.sharding import PartitionSpec as P

MESH = pl.DeviceIdType.MESH
NH = 2
BF16 = jnp.bfloat16
F32 = jnp.float32


def kernel(
    ns, nz, tok, dim, ff,
    x_hbm, y_hbm, wg_hbm, wu_hbm, wd_hbm, mg_ref, mu_ref, md_ref,
    gin, ng_ref, nu_ref, nd_ref,
    xb, yb, wgb, wub, wdb, act, act_t, pre, part, ring, dxb, out1, late,
    in_sem, ring_send, ring_recv, dx_send, dx_recv, zero_sem, late_send, late_recv,
):
    sec = lax.axis_index("section")
    dp = lax.axis_index("dp")
    half = dp // nz
    z = dp % nz
    width = dim // (NH * nz)
    three = 3 * ff
    far = nz // 2
    mirror = ns - 1 - sec
    total_rows = tok * NH * nz

    def at_z(distance):
        return (z + distance + nz) % nz

    def device(s, h, zz):
        return (s, h * nz + zz)

    loads = []
    for b in (1, 0):
        for n, (src, dst) in enumerate(
            ((x_hbm, xb), (wg_hbm, wgb), (wu_hbm, wub), (y_hbm, yb), (wd_hbm, wdb))
        ):
            copy = pltpu.make_async_copy(src.at[0, b], dst.at[b], in_sem.at[b, n])
            copy.start()
            loads.append(copy)

    def load(b, n, src, dst):
        return pltpu.make_async_copy(src.at[0, b], dst.at[b], in_sem.at[b, n])

    barrier = pltpu.get_barrier_semaphore()
    neighbours = [
        device(sec, half, at_z(1)),
        device(sec, half, at_z(-1)),
        device(mirror, 0, z),
        device(mirror, 1, z),
        device(sec, 1 - half, z),
        device((sec + 1) % ns, half, z),
        device((sec + ns - 1) % ns, half, z),
    ]
    for target in neighbours:
        pl.semaphore_signal(barrier, inc=1, device_id=target, device_id_type=MESH)

    def forward(i, carry):
        b = 1 - i
        load(b, 0, x_hbm, xb).wait()
        load(b, 1, wg_hbm, wgb).wait()
        pre[0] = jnp.dot(xb[b], wgb[b], preferred_element_type=F32)
        load(b, 2, wu_hbm, wub).wait()
        pre[1] = jnp.dot(xb[b], wub[b], preferred_element_type=F32)
        load(b, 3, y_hbm, yb).wait()
        load(b, 4, wd_hbm, wdb).wait()
        pre[2] = lax.dot_general(
            yb[b], wdb[b], (((1,), (1,)), ((), ())), preferred_element_type=F32
        )
        step = min(128, tok)
        for row in range(0, tok, step):
            rows = pl.ds(row, step)
            gpre, upre, dhid = pre[0, rows, :], pre[1, rows, :], pre[2, rows, :]
            sig = jax.nn.sigmoid(gpre)
            activated = gpre * sig
            dgate = dhid * upre * sig * (1.0 + gpre * (1.0 - sig))
            dup = dhid * activated
            hidden = activated * upre
            act[b, 0, rows, :] = dgate.astype(BF16)
            act[b, 1, rows, :] = dup.astype(BF16)
            act_t[b, 0:ff, rows] = dgate.T.astype(BF16)
            act_t[b, ff : 2 * ff, rows] = dup.T.astype(BF16)
            act_t[b, 2 * ff : three, rows] = hidden.T.astype(BF16)
        return carry

    def weight_grad(b, h, pair):
        start = pl.multiple_of((h * nz + 2 * pair) * width, 2 * width)
        cols = pl.ds(start, 2 * width)
        gate_up = jnp.dot(act_t[b, 0 : 2 * ff, :], xb[b, :, cols], preferred_element_type=F32)
        part[b, h, 2 * pair, 0 : 2 * ff, :] = gate_up[:, :width].astype(BF16)
        part[b, h, 2 * pair + 1, 0 : 2 * ff, :] = gate_up[:, width:].astype(BF16)
        down = jnp.dot(act_t[b, 2 * ff : three, :], yb[b, :, cols], preferred_element_type=F32)
        part[b, h, 2 * pair, 2 * ff : three, :] = down[:, :width].astype(BF16)
        part[b, h, 2 * pair + 1, 2 * ff : three, :] = down[:, width:].astype(BF16)

    def message(direction, h, d, b):
        sign = -1 if direction == 0 else 1
        return pltpu.make_async_remote_copy(
            src_ref=part.at[b, h, at_z(sign * d)],
            dst_ref=ring.at[direction, h, d - 1, b],
            send_sem=ring_send.at[direction, h, d - 1, b],
            recv_sem=ring_recv.at[direction, h, d - 1, b],
            device_id=device(sec, half, at_z(sign)),
            device_id_type=MESH,
        )

    def accumulate(direction, h, d, b):
        sign = -1 if direction == 0 else 1
        message(direction, h, d + 1, b).wait_recv()
        target = at_z(sign * d)
        mine = part[b, h, target].astype(F32)
        part[b, h, target] = (mine + ring[direction, h, d, b].astype(F32)).astype(BF16)

    long = ((0, 0), (1, 1))
    short = ((0, 1), (1, 0))

    half_z = z // 2
    pairs = nz // 2
    first_pair = (half_z + far // 2) % pairs

    for i in range(2):
        b = 1 - i
        forward(i, 0)
        for h in range(NH):
            weight_grad(b, h, first_pair)
        if i == 0:
            pl.semaphore_wait(barrier, len(neighbours))
        for direction, h in long:
            message(direction, h, far, b).start()

    def rest(j, carry):
        pair = (half_z + far // 2 + 1 + j) % pairs
        for b in (1, 0):
            for h in range(NH):
                weight_grad(b, h, pair)
        return carry

    lax.fori_loop(0, pairs - 1, rest, 0)
    if far > 1:
        for b in (1, 0):
            for direction, h in short:
                message(direction, h, far - 1, b).start()

    def dx_copy(b):
        step = -1 if b == 0 else 1
        return pltpu.make_async_remote_copy(
            src_ref=dxb.at[b],
            dst_ref=gin.at[0, b],
            send_sem=dx_send.at[b],
            recv_sem=dx_recv.at[b],
            device_id=device(sec + step, half, z),
            device_id_type=MESH,
        )

    def zero_copy(b):
        return pltpu.make_async_copy(dxb.at[b], gin.at[0, 1 - b], zero_sem)

    cut = 2 * width
    for b in (1, 0):

        def dx_chunk(j, carry, b=b):
            cols = pl.ds(pl.multiple_of(j * cut, cut), cut)
            contract = (((1,), (1,)), ((), ()))
            dx = lax.dot_general(
                act[b, 0], wgb[b, cols, :], contract, preferred_element_type=F32
            ) + lax.dot_general(act[b, 1], wub[b, cols, :], contract, preferred_element_type=F32)
            dxb[b, :, cols] = dx.astype(BF16)
            return carry

        sends = sec > 0 if b == 0 else sec < ns - 1

        @pl.when(sends)
        def _(b=b, dx_chunk=dx_chunk):
            lax.fori_loop(0, dim // cut, dx_chunk, 0)
            dx_copy(b).start()

        @pl.when(jnp.logical_not(sends))
        def _(b=b):
            dxb[b] = jnp.zeros((tok, dim), BF16)
            zero_copy(b).start()

    for d in range(far - 1, 0, -1):
        for b in (1, 0):
            for direction, h in long:
                accumulate(direction, h, d, b)
                message(direction, h, d, b).start()
        if d > 1:
            for b in (1, 0):
                for direction, h in short:
                    accumulate(direction, h, d - 1, b)
                    message(direction, h, d - 1, b).start()

    def reduced(b, h):
        return (
            part[b, h, z].astype(F32)
            + ring[0, h, 0, b].astype(F32)
            + ring[1, h, 0, b].astype(F32)
        )

    def finish_wait(b, h):
        message(0, h, 1, b).wait_recv()
        message(1, h, 1, b).wait_recv()

    def late_copy(n):
        if n < NH:
            target, slot = device(mirror, n, z), half
        else:
            target, slot = device(sec, 1 - half, z), NH
        return pltpu.make_async_remote_copy(
            src_ref=out1.at[n],
            dst_ref=late.at[slot],
            send_sem=late_send.at[n],
            recv_sem=late_recv.at[slot],
            device_id=target,
            device_id_type=MESH,
        )

    for h in range(NH):
        finish_wait(1, h)
        out1[h] = reduced(1, h).astype(BF16)
        late_copy(h).start()
    for h in range(NH):
        finish_wait(0, h)
    out1[NH] = reduced(0, 1 - half).astype(BF16)
    late_copy(NH).start()

    def late_wait(slot):
        pltpu.make_async_remote_copy(
            src_ref=out1.at[0],
            dst_ref=late.at[slot],
            send_sem=late_send.at[0],
            recv_sem=late_recv.at[slot],
            device_id=device(mirror, 0, z),
            device_id_type=MESH,
        ).wait_recv()

    for slot in range(3):
        late_wait(slot)
    scale = 1.0 / float(total_rows) ** 0.5
    for n, (mom, new) in enumerate(((mg_ref, ng_ref), (mu_ref, nu_ref), (md_ref, nd_ref))):
        rows = pl.ds(n * ff, ff)
        total = (
            part[0, half, z, rows, :].astype(F32)
            + ring[0, half, 0, 0, rows, :].astype(F32)
            + ring[1, half, 0, 0, rows, :].astype(F32)
        )
        for slot in range(3):
            total = total + late[slot, rows, :].astype(F32)
        new[0] = 0.9 * mom[0] + total.T * scale

    for h in range(NH):
        late_copy(h).wait_send()
    late_copy(NH).wait_send()
    for b in range(2):
        for d in range(1, far + 1):
            for direction, h in long + (short if d < far else ()):
                message(direction, h, d, b).wait_send()

    @pl.when(sec > 0)
    def _():
        dx_copy(0).wait_send()
        dx_copy(1).wait_recv()

    @pl.when(sec < ns - 1)
    def _():
        dx_copy(1).wait_send()
        dx_copy(0).wait_recv()

    @pl.when(sec == 0)
    def _():
        zero_copy(0).wait()

    @pl.when(sec == ns - 1)
    def _():
        zero_copy(1).wait()


def body(inputs, cotangent, w_gate, w_up, w_down, mom_gate, mom_up, mom_down):
    ns = lax.axis_size("section")
    nz = lax.axis_size("dp") // NH
    _, _, tok, dim = inputs.shape
    ff = w_gate.shape[-1]
    far = nz // 2
    width = dim // (NH * nz)
    anywhere = pl.BlockSpec(memory_space=pl.ANY)
    vmem = pl.BlockSpec(memory_space=pltpu.VMEM)
    dma = pltpu.SemaphoreType.DMA
    return pl.pallas_call(
        functools.partial(kernel, ns, nz, tok, dim, ff),
        out_shape=(
            jax.ShapeDtypeStruct(inputs.shape, BF16),
            jax.ShapeDtypeStruct(mom_gate.shape, F32),
            jax.ShapeDtypeStruct(mom_up.shape, F32),
            jax.ShapeDtypeStruct(mom_down.shape, F32),
        ),
        in_specs=[anywhere] * 5 + [vmem] * 3,
        out_specs=(anywhere, vmem, vmem, vmem),
        scratch_shapes=[
            pltpu.VMEM((2, tok, dim), BF16),
            pltpu.VMEM((2, tok, dim), BF16),
            pltpu.VMEM((2, dim, ff), BF16),
            pltpu.VMEM((2, dim, ff), BF16),
            pltpu.VMEM((2, ff, dim), BF16),
            pltpu.VMEM((2, 2, tok, ff), BF16),
            pltpu.VMEM((2, 3 * ff, tok), BF16),
            pltpu.VMEM((3, tok, ff), F32),
            pltpu.VMEM((2, NH, nz, 3 * ff, width), BF16),
            pltpu.VMEM((2, NH, far, 2, 3 * ff, width), BF16),
            pltpu.VMEM((2, tok, dim), BF16),
            pltpu.VMEM((NH + 1, 3 * ff, width), BF16),
            pltpu.VMEM((3, 3 * ff, width), BF16),
            dma((2, 5)),
            dma((2, NH, far, 2)),
            dma((2, NH, far, 2)),
            dma((2,)),
            dma((2,)),
            dma,
            dma((NH + 1,)),
            dma((3,)),
        ],
        compiler_params=pltpu.CompilerParams(
            collective_id=0, has_side_effects=True, vmem_limit_bytes=56 * 2**20
        ),
        name="relay_step",
    )(inputs, cotangent, w_gate, w_up, w_down, mom_gate, mom_up, mom_down)


def solution(mesh):
    placed = (
        P("section", None, "dp", None),
        P("section", None, "dp", None),
        P("section", None, None, None),
        P("section", None, None, None),
        P("section", None, None, None),
        P("section", "dp", None),
        P("section", "dp", None),
        P("section", "dp", None),
    )
    return jax.shard_map(
        body,
        mesh=mesh,
        in_specs=placed,
        out_specs=(
            P("section", None, "dp", None),
            P("section", "dp", None),
            P("section", "dp", None),
            P("section", "dp", None),
        ),
        check_vma=False,
    )
```

time: 880 us -> 89.9 us (0.10)
  waiting for transfers between devices: 813 us -> 0 us
  Pallas kernels: 0 us -> 84 us
  matrix products: 18.7 us -> 0 us
  between operations: 14 us -> 0.67 us
  starting transfers between devices: 11.7 us -> 0 us
    reduce_scatter x3 -> x0, waiting for transfers between devices: 584 us -> none  [the longest x1 210 us: body(): lax.psum_scatter(first[3] + mirrored[2], 'dp', scatter_dimension=0, tiled...]
    ppermute x6 -> x0, waiting for transfers between devices: 228 us -> none  [the longest x4 210 us: from_partner(): return lax.ppermute(value, axis, pairs)]
    pallas_call x0 -> x1, Pallas kernels: none -> 84 us  [body(): pl.pallas_call(functools.partial(kernel, ns, nz, tok, dim, ff), out_shape...]
    dot_general x16 -> x0, matrix products: 18.7 us -> none  [the longest x6 10.1 us: contract_rows(): lax.dot_general(left, right, (((0,), (0,)), ((), ())), preferred_element_...]
    ppermute x6 -> x0, starting transfers between devices: 11.5 us -> none  [the longest x2 7.2 us: from_behind(): lax.ppermute(value, axis, [(source, source + steps) for source in range(f...]
  transfers between devices with their start and end apart: 9 -> 0, of which waited for: 9 -> 0; matrix products, arithmetic and copies ran while one was open for 2% -> 0% of each run, Pallas kernels for 0% -> 0%
where the time goes in v1:
time: 89.9 us; the launch traced here: 89.8 us
  Pallas kernels  84 us (93%)
  local copies, waits for them, and re-layouts  5.19 us (6%)
    pallas_call x1, Pallas kernels, body(): pl.pallas_call(functools.partial(kernel, ns, nz, tok, dim, ff), out_shape...  84 us
    unnamed x10, local copies, waits for them, and re-layouts  5.19 us

profile of v1, /device:TPU:1, one launch (start us, length us, event | category | flops | bytes accessed | tf_op | source)
XLA Modules:
  0.0 89.8 jit_solution(6921737251654052474)
XLA Ops:
  0.6 84.0 %relay_step.1 = (bf16[1,2,256,2048]{3,2,1,0:T(8,128)(2,1)}, f32[1,128,256]{2,1,0:T(8,128)}, f32[1,128,256]{2,1,0:T(8,128)}, f32[1,128,256]{2,1,0:T(8,128)}) custom-call(bf16[1,2,256,2048]{3,2,1,0:T(8,128)(2,1)} %x_hbm.1, bf16[1,2,256,2048]{3,2,1,0:T(8,128)(2,1)} %y_hbm.1, bf16[1,2,2048,256]{3,2,1,0:T(8,128)(2,1)} %wg_hbm.1, ...), custom_call_target="tpu_custom_call" | custom-call | tf_op jit(solution)/shard_map/relay_step/pallas_call | solution.py:294
  84.6 0.0 copy-start.2
  84.6 0.0 copy-start.1
  84.6 0.0 copy-start
  84.6 3.2 %copy.16 = bf16[1,2,256,2048]{3,2,1,0:T(8,128)(2,1)} copy(bf16[1,2,256,2048]{3,2,1,0:T(8,128)(2,1)} %get-tuple-element.8) | data formatting | bytes 4194304
  87.8 0.0 copy-done.2
  87.8 0.7 copy.17
  88.5 0.0 copy-done.1
  88.5 0.7 copy.18
  89.2 0.0 copy-done
  89.2 0.7 copy.19
Async XLA Ops:
  84.6 3.2 %copy-start.2 = (f32[1,128,256]{2,1,0:T(8,128)S(1)}, f32[1,128,256]{2,1,0:T(8,128)}, u32[]{:S(2)}) copy-start(f32[1,128,256]{2,1,0:T(8,128)} %get-tuple-element.9) | copy-start | bytes 393220
  84.6 3.9 %copy-start.1 = (f32[1,128,256]{2,1,0:T(8,128)S(1)}, f32[1,128,256]{2,1,0:T(8,128)}, u32[]{:S(2)}) copy-start(f32[1,128,256]{2,1,0:T(8,128)} %get-tuple-element.10) | copy-start | bytes 393220
  84.6 4.5 %copy-start = (f32[1,128,256]{2,1,0:T(8,128)S(1)}, f32[1,128,256]{2,1,0:T(8,128)}, u32[]{:S(2)}) copy-start(f32[1,128,256]{2,1,0:T(8,128)} %get-tuple-element.11) | copy-start | bytes 393220

commit v2 on v1

--- a/solution.py
+++ b/solution.py
@@ -9,16 +9,19 @@
 
 MESH = pl.DeviceIdType.MESH
 NH = 2
+CROSS = 0.25
 BF16 = jnp.bfloat16
 F32 = jnp.float32
 
 
 def kernel(
-    ns, nz, tok, dim, ff,
+    ns, nz, tok, dim, ff, cross,
     x_hbm, y_hbm, wg_hbm, wu_hbm, wd_hbm, mg_ref, mu_ref, md_ref,
     gin, ng_ref, nu_ref, nd_ref,
     xb, yb, wgb, wub, wdb, act, act_t, pre, part, ring, dxb, out1, late,
+    wide, wide_in, wide_ring,
     in_sem, ring_send, ring_recv, dx_send, dx_recv, zero_sem, late_send, late_recv,
+    wide_send, wide_recv, wide_ring_send, wide_ring_recv,
 ):
     sec = lax.axis_index("section")
     dp = lax.axis_index("dp")
@@ -26,6 +29,7 @@
     z = dp % nz
     width = dim // (NH * nz)
     three = 3 * ff
+    keep = three - cross
     far = nz // 2
     mirror = ns - 1 - sec
     total_rows = tok * NH * nz
@@ -96,8 +100,62 @@
         part[b, h, 2 * pair, 0 : 2 * ff, :] = gate_up[:, :width].astype(BF16)
         part[b, h, 2 * pair + 1, 0 : 2 * ff, :] = gate_up[:, width:].astype(BF16)
         down = jnp.dot(act_t[b, 2 * ff : three, :], yb[b, :, cols], preferred_element_type=F32)
-        part[b, h, 2 * pair, 2 * ff : three, :] = down[:, :width].astype(BF16)
-        part[b, h, 2 * pair + 1, 2 * ff : three, :] = down[:, width:].astype(BF16)
+        for n in range(2):
+            tile = down[:, n * width : (n + 1) * width].astype(BF16)
+            if keep > 2 * ff:
+                part[b, h, 2 * pair + n, 2 * ff : keep, :] = tile[: keep - 2 * ff]
+            wide[b, h, 2 * pair + n] = tile[keep - 2 * ff :]
+
+    def wide_copy(n):
+        if n < NH:
+            src, target, slot = wide.at[1, n], device(mirror, n, z), half
+        else:
+            src, target, slot = wide.at[0, 1 - half], device(sec, 1 - half, z), NH
+        return pltpu.make_async_remote_copy(
+            src_ref=src,
+            dst_ref=wide_in.at[slot],
+            send_sem=wide_send.at[n],
+            recv_sem=wide_recv.at[slot],
+            device_id=target,
+            device_id_type=MESH,
+        )
+
+    def wide_wait(slot):
+        pltpu.make_async_remote_copy(
+            src_ref=wide.at[1, 0],
+            dst_ref=wide_in.at[slot],
+            send_sem=wide_send.at[0],
+            recv_sem=wide_recv.at[slot],
+            device_id=device(mirror, 0, z),
+            device_id_type=MESH,
+        ).wait_recv()
+
+    part_rows = cross // 2
+
+    def wide_message(direction, g, d):
+        sign = -1 if direction == 0 else 1
+        return pltpu.make_async_remote_copy(
+            src_ref=wide.at[0, half, at_z(sign * d), pl.ds(g * part_rows, part_rows)],
+            dst_ref=wide_ring.at[direction, g, d - 1],
+            send_sem=wide_ring_send.at[direction, g, d - 1],
+            recv_sem=wide_ring_recv.at[direction, g, d - 1],
+            device_id=device(sec, half, at_z(sign)),
+            device_id_type=MESH,
+        )
+
+    def wide_sum(target):
+        total = wide[0, half, target].astype(F32)
+        for slot in range(NH + 1):
+            total = total + wide_in[slot, target].astype(F32)
+        wide[0, half, target] = total.astype(BF16)
+
+    def wide_accumulate(direction, g, d):
+        sign = -1 if direction == 0 else 1
+        wide_message(direction, g, d + 1).wait_recv()
+        target = at_z(sign * d)
+        rows = pl.ds(g * part_rows, part_rows)
+        mine = wide[0, half, target, rows, :].astype(F32)
+        wide[0, half, target, rows, :] = (mine + wide_ring[direction, g, d].astype(F32)).astype(BF16)
 
     def message(direction, h, d, b):
         sign = -1 if direction == 0 else 1
@@ -134,16 +192,19 @@
         for direction, h in long:
             message(direction, h, far, b).start()
 
-    def rest(j, carry):
-        pair = (half_z + far // 2 + 1 + j) % pairs
-        for b in (1, 0):
+        def rest(j, carry, b=b):
+            pair = (half_z + far // 2 + 1 + j) % pairs
             for h in range(NH):
                 weight_grad(b, h, pair)
-        return carry
-
-    lax.fori_loop(0, pairs - 1, rest, 0)
-    if far > 1:
-        for b in (1, 0):
+            return carry
+
+        lax.fori_loop(0, pairs - 1, rest, 0)
+        if b == 1:
+            wide_copy(0).start()
+            wide_copy(1).start()
+        else:
+            wide_copy(NH).start()
+        if far > 1:
             for direction, h in short:
                 message(direction, h, far - 1, b).start()
 
@@ -185,16 +246,40 @@
             dxb[b] = jnp.zeros((tok, dim), BF16)
             zero_copy(b).start()
 
-    for d in range(far - 1, 0, -1):
+    def ring_step(lanes, d):
         for b in (1, 0):
-            for direction, h in long:
+            for direction, h in lanes:
                 accumulate(direction, h, d, b)
                 message(direction, h, d, b).start()
+
+    def wide_start():
+        for slot in range(NH + 1):
+            wide_wait(slot)
+        for d in range(far, -1, -1):
+            for sign in (-1, 1) if 0 < d < far else (1,):
+                wide_sum(at_z(sign * d))
+            if d == far:
+                for direction, g in long:
+                    wide_message(direction, g, far).start()
+            elif d == far - 1 and d > 0:
+                for direction, g in short:
+                    wide_message(direction, g, d).start()
+
+    def wide_step(lanes, d):
+        for direction, g in lanes:
+            wide_accumulate(direction, g, d)
+            wide_message(direction, g, d).start()
+
+    for d in range(far - 1, 0, -1):
+        if d == 1:
+            wide_start()
+        ring_step(long, d)
         if d > 1:
-            for b in (1, 0):
-                for direction, h in short:
-                    accumulate(direction, h, d - 1, b)
-                    message(direction, h, d - 1, b).start()
+            ring_step(short, d - 1)
+    for d in range(far - 1, 0, -1):
+        wide_step(long, d)
+        if d > 1:
+            wide_step(short, d - 1)
 
     def reduced(b, h):
         return (
@@ -243,8 +328,12 @@
     for slot in range(3):
         late_wait(slot)
     scale = 1.0 / float(total_rows) ** 0.5
-    for n, (mom, new) in enumerate(((mg_ref, ng_ref), (mu_ref, nu_ref), (md_ref, nd_ref))):
-        rows = pl.ds(n * ff, ff)
+    for direction in range(2):
+        for g in range(2):
+            wide_message(direction, g, 1).wait_recv()
+
+    def total_of(lo, hi):
+        rows = pl.ds(lo, hi - lo)
         total = (
             part[0, half, z, rows, :].astype(F32)
             + ring[0, half, 0, 0, rows, :].astype(F32)
@@ -252,11 +341,28 @@
         )
         for slot in range(3):
             total = total + late[slot, rows, :].astype(F32)
+        return total
+
+    pieces = [total_of(2 * ff, keep)] if keep > 2 * ff else []
+    for g in range(2):
+        rows = pl.ds(g * part_rows, part_rows)
+        pieces.append(
+            wide[0, half, z, rows, :].astype(F32)
+            + wide_ring[0, g, 0].astype(F32)
+            + wide_ring[1, g, 0].astype(F32)
+        )
+    totals = (total_of(0, ff), total_of(ff, 2 * ff), jnp.concatenate(pieces, axis=0))
+    for total, mom, new in zip(totals, (mg_ref, mu_ref, md_ref), (ng_ref, nu_ref, nd_ref)):
         new[0] = 0.9 * mom[0] + total.T * scale
 
     for h in range(NH):
         late_copy(h).wait_send()
     late_copy(NH).wait_send()
+    for n in range(NH + 1):
+        wide_copy(n).wait_send()
+    for d in range(1, far + 1):
+        for direction, g in long + (short if d < far else ()):
+            wide_message(direction, g, d).wait_send()
     for b in range(2):
         for d in range(1, far + 1):
             for direction, h in long + (short if d < far else ()):
@@ -288,11 +394,13 @@
     ff = w_gate.shape[-1]
     far = nz // 2
     width = dim // (NH * nz)
+    cross = int(3 * ff * CROSS) // 32 * 32
+    keep = 3 * ff - cross
     anywhere = pl.BlockSpec(memory_space=pl.ANY)
     vmem = pl.BlockSpec(memory_space=pltpu.VMEM)
     dma = pltpu.SemaphoreType.DMA
     return pl.pallas_call(
-        functools.partial(kernel, ns, nz, tok, dim, ff),
+        functools.partial(kernel, ns, nz, tok, dim, ff, cross),
         out_shape=(
             jax.ShapeDtypeStruct(inputs.shape, BF16),
             jax.ShapeDtypeStruct(mom_gate.shape, F32),
@@ -310,11 +418,14 @@
             pltpu.VMEM((2, 2, tok, ff), BF16),
             pltpu.VMEM((2, 3 * ff, tok), BF16),
             pltpu.VMEM((3, tok, ff), F32),
-            pltpu.VMEM((2, NH, nz, 3 * ff, width), BF16),
-            pltpu.VMEM((2, NH, far, 2, 3 * ff, width), BF16),
+            pltpu.VMEM((2, NH, nz, keep, width), BF16),
+            pltpu.VMEM((2, NH, far, 2, keep, width), BF16),
             pltpu.VMEM((2, tok, dim), BF16),
-            pltpu.VMEM((NH + 1, 3 * ff, width), BF16),
-            pltpu.VMEM((3, 3 * ff, width), BF16),
+            pltpu.VMEM((NH + 1, keep, width), BF16),
+            pltpu.VMEM((NH + 1, keep, width), BF16),
+            pltpu.VMEM((2, NH, nz, cross, width), BF16),
+            pltpu.VMEM((NH + 1, nz, cross, width), BF16),
+            pltpu.VMEM((2, 2, far, cross // 2, width), BF16),
             dma((2, 5)),
             dma((2, NH, far, 2)),
             dma((2, NH, far, 2)),
@@ -322,7 +433,11 @@
             dma((2,)),
             dma,
             dma((NH + 1,)),
-            dma((3,)),
+            dma((NH + 1,)),
+            dma((NH + 1,)),
+            dma((NH + 1,)),
+            dma((2, 2, far)),
+            dma((2, 2, far)),
         ],
         compiler_params=pltpu.CompilerParams(
             collective_id=0, has_side_effects=True, vmem_limit_bytes=56 * 2**20

time: 89.9 us -> 78.8 us (0.88)
  Pallas kernels: 84 us -> 72.8 us
    pallas_call x1, Pallas kernels: 84 us -> 72.8 us  [body(): pl.pallas_call(functools.partial(kernel, ns, nz, tok, dim, ff, cross), ou...]
where the time goes in v2:
time: 78.8 us; the launch traced here: 78.6 us
  Pallas kernels  72.8 us (92%)
  local copies, waits for them, and re-layouts  5.19 us (7%)
    pallas_call x1, Pallas kernels, body(): pl.pallas_call(functools.partial(kernel, ns, nz, tok, dim, ff, cross), ou...  72.8 us
    unnamed x10, local copies, waits for them, and re-layouts  5.19 us

profile of v2, /device:TPU:1, one launch (start us, length us, event | category | flops | bytes accessed | tf_op | source)
XLA Modules:
  0.0 78.6 jit_solution(9073162065597791831)
XLA Ops:
  0.6 72.8 %relay_step.1 = (bf16[1,2,256,2048]{3,2,1,0:T(8,128)(2,1)}, f32[1,128,256]{2,1,0:T(8,128)}, f32[1,128,256]{2,1,0:T(8,128)}, f32[1,128,256]{2,1,0:T(8,128)}) custom-call(bf16[1,2,256,2048]{3,2,1,0:T(8,128)(2,1)} %x_hbm.1, bf16[1,2,256,2048]{3,2,1,0:T(8,128)(2,1)} %y_hbm.1, bf16[1,2,2048,256]{3,2,1,0:T(8,128)(2,1)} %wg_hbm.1, ...), custom_call_target="tpu_custom_call" | custom-call | tf_op jit(solution)/shard_map/relay_step/pallas_call | solution.py:402
  73.4 0.0 copy-start.2
  73.4 0.0 copy-start.1
  73.4 0.0 copy-start
  73.4 3.2 %copy.16 = bf16[1,2,256,2048]{3,2,1,0:T(8,128)(2,1)} copy(bf16[1,2,256,2048]{3,2,1,0:T(8,128)(2,1)} %get-tuple-element.8) | data formatting | bytes 4194304
  76.6 0.0 copy-done.2
  76.6 0.7 copy.17
  77.3 0.0 copy-done.1
  77.3 0.7 copy.18
  78.0 0.0 copy-done
  78.0 0.7 copy.19
Async XLA Ops:
  73.4 3.2 %copy-start.2 = (f32[1,128,256]{2,1,0:T(8,128)S(1)}, f32[1,128,256]{2,1,0:T(8,128)}, u32[]{:S(2)}) copy-start(f32[1,128,256]{2,1,0:T(8,128)} %get-tuple-element.9) | copy-start | bytes 393220
  73.4 3.9 %copy-start.1 = (f32[1,128,256]{2,1,0:T(8,128)S(1)}, f32[1,128,256]{2,1,0:T(8,128)}, u32[]{:S(2)}) copy-start(f32[1,128,256]{2,1,0:T(8,128)} %get-tuple-element.10) | copy-start | bytes 393220
  73.4 4.5 %copy-start = (f32[1,128,256]{2,1,0:T(8,128)S(1)}, f32[1,128,256]{2,1,0:T(8,128)}, u32[]{:S(2)}) copy-start(f32[1,128,256]{2,1,0:T(8,128)} %get-tuple-element.11) | copy-start | bytes 393220

commit v3 on v2

--- a/solution.py
+++ b/solution.py
@@ -16,8 +16,8 @@
 
 def kernel(
     ns, nz, tok, dim, ff, cross,
-    x_hbm, y_hbm, wg_hbm, wu_hbm, wd_hbm, mg_ref, mu_ref, md_ref,
-    gin, ng_ref, nu_ref, nd_ref,
+    x_hbm, y_hbm, wg_hbm, wu_hbm, wd_hbm,
+    gin, total_ref,
     xb, yb, wgb, wub, wdb, act, act_t, pre, part, ring, dxb, out1, late,
     wide, wide_in, wide_ring,
     in_sem, ring_send, ring_recv, dx_send, dx_recv, zero_sem, late_send, late_recv,
@@ -31,8 +31,8 @@
     three = 3 * ff
     keep = three - cross
     far = nz // 2
+    pairs = nz // 2
     mirror = ns - 1 - sec
-    total_rows = tok * NH * nz
 
     def at_z(distance):
         return (z + distance + nz) % nz
@@ -106,26 +106,33 @@
                 part[b, h, 2 * pair + n, 2 * ff : keep, :] = tile[: keep - 2 * ff]
             wide[b, h, 2 * pair + n] = tile[keep - 2 * ff :]
 
-    def wide_copy(n):
+    def pair_at(piece):
+        if pairs == 4:
+            piece = (0, 3 - 2 * (z % 2), 1 + 2 * (z % 2), 2)[piece]
+        return (z // 2 + far // 2 + piece) % pairs
+
+    def wide_copy(n, piece):
+        cols = pl.ds(2 * pair_at(piece), 2)
         if n < NH:
-            src, target, slot = wide.at[1, n], device(mirror, n, z), half
+            src, target, slot = wide.at[1, n, cols], device(mirror, n, z), half
         else:
-            src, target, slot = wide.at[0, 1 - half], device(sec, 1 - half, z), NH
+            src, target, slot = wide.at[0, 1 - half, cols], device(sec, 1 - half, z), NH
         return pltpu.make_async_remote_copy(
             src_ref=src,
-            dst_ref=wide_in.at[slot],
-            send_sem=wide_send.at[n],
-            recv_sem=wide_recv.at[slot],
+            dst_ref=wide_in.at[slot, cols],
+            send_sem=wide_send.at[n, piece],
+            recv_sem=wide_recv.at[slot, piece],
             device_id=target,
             device_id_type=MESH,
         )
 
-    def wide_wait(slot):
+    def wide_wait(slot, piece):
+        cols = pl.ds(2 * pair_at(piece), 2)
         pltpu.make_async_remote_copy(
-            src_ref=wide.at[1, 0],
-            dst_ref=wide_in.at[slot],
-            send_sem=wide_send.at[0],
-            recv_sem=wide_recv.at[slot],
+            src_ref=wide.at[1, 0, cols],
+            dst_ref=wide_in.at[slot, cols],
+            send_sem=wide_send.at[0, piece],
+            recv_sem=wide_recv.at[slot, piece],
             device_id=device(mirror, 0, z),
             device_id_type=MESH,
         ).wait_recv()
@@ -178,36 +185,6 @@
     long = ((0, 0), (1, 1))
     short = ((0, 1), (1, 0))
 
-    half_z = z // 2
-    pairs = nz // 2
-    first_pair = (half_z + far // 2) % pairs
-
-    for i in range(2):
-        b = 1 - i
-        forward(i, 0)
-        for h in range(NH):
-            weight_grad(b, h, first_pair)
-        if i == 0:
-            pl.semaphore_wait(barrier, len(neighbours))
-        for direction, h in long:
-            message(direction, h, far, b).start()
-
-        def rest(j, carry, b=b):
-            pair = (half_z + far // 2 + 1 + j) % pairs
-            for h in range(NH):
-                weight_grad(b, h, pair)
-            return carry
-
-        lax.fori_loop(0, pairs - 1, rest, 0)
-        if b == 1:
-            wide_copy(0).start()
-            wide_copy(1).start()
-        else:
-            wide_copy(NH).start()
-        if far > 1:
-            for direction, h in short:
-                message(direction, h, far - 1, b).start()
-
     def dx_copy(b):
         step = -1 if b == 0 else 1
         return pltpu.make_async_remote_copy(
@@ -223,9 +200,9 @@
         return pltpu.make_async_copy(dxb.at[b], gin.at[0, 1 - b], zero_sem)
 
     cut = 2 * width
-    for b in (1, 0):
-
-        def dx_chunk(j, carry, b=b):
+
+    def input_grad(b):
+        def dx_chunk(j, carry):
             cols = pl.ds(pl.multiple_of(j * cut, cut), cut)
             contract = (((1,), (1,)), ((), ()))
             dx = lax.dot_general(
@@ -237,49 +214,110 @@
         sends = sec > 0 if b == 0 else sec < ns - 1
 
         @pl.when(sends)
-        def _(b=b, dx_chunk=dx_chunk):
+        def _():
             lax.fori_loop(0, dim // cut, dx_chunk, 0)
             dx_copy(b).start()
 
         @pl.when(jnp.logical_not(sends))
-        def _(b=b):
+        def _():
             dxb[b] = jnp.zeros((tok, dim), BF16)
             zero_copy(b).start()
 
-    def ring_step(lanes, d):
-        for b in (1, 0):
-            for direction, h in lanes:
-                accumulate(direction, h, d, b)
-                message(direction, h, d, b).start()
-
-    def wide_start():
+    def ring_step(lanes, d, b):
+        for direction, h in lanes:
+            accumulate(direction, h, d, b)
+            message(direction, h, d, b).start()
+
+    def long_step(d, b):
+        ring_step(long, d, b)
+
+    def short_step(d, b):
+        if d > 0:
+            ring_step(short, d, b)
+
+    def block(b, between):
+        forward(1 - b, 0)
+        for piece in range(pairs):
+            pair = pair_at(piece)
+            for h in range(NH):
+                weight_grad(b, h, pair)
+            if piece == 0:
+                if b == 1:
+                    pl.semaphore_wait(barrier, len(neighbours))
+                for direction, h in long:
+                    message(direction, h, far, b).start()
+            if piece == 1 and far > 1:
+                for direction, h in short:
+                    message(direction, h, far - 1, b).start()
+            for n in (0, 1) if b == 1 else (NH,):
+                wide_copy(n, piece).start()
+            between(piece)
+
+    def wide_first():
         for slot in range(NH + 1):
-            wide_wait(slot)
-        for d in range(far, -1, -1):
-            for sign in (-1, 1) if 0 < d < far else (1,):
+            wide_wait(slot, 0)
+        wide_sum(at_z(far))
+        for direction, g in long:
+            wide_message(direction, g, far).start()
+
+    def wide_second():
+        for slot in range(NH + 1):
+            wide_wait(slot, 1)
+        for sign in (-1, 1):
+            wide_sum(at_z(sign * (far - 1)))
+        for direction, g in short:
+            wide_message(direction, g, far - 1).start()
+
+    def wide_others():
+        for piece in range(2, pairs):
+            for slot in range(NH + 1):
+                wide_wait(slot, piece)
+        for d in range(far - 2, -1, -1):
+            for sign in (-1, 1) if d > 0 else (1,):
                 wide_sum(at_z(sign * d))
-            if d == far:
-                for direction, g in long:
-                    wide_message(direction, g, far).start()
-            elif d == far - 1 and d > 0:
-                for direction, g in short:
-                    wide_message(direction, g, d).start()
 
     def wide_step(lanes, d):
         for direction, g in lanes:
             wide_accumulate(direction, g, d)
             wide_message(direction, g, d).start()
 
-    for d in range(far - 1, 0, -1):
-        if d == 1:
-            wide_start()
-        ring_step(long, d)
-        if d > 1:
-            ring_step(short, d - 1)
-    for d in range(far - 1, 0, -1):
-        wide_step(long, d)
-        if d > 1:
-            wide_step(short, d - 1)
+    if far == 4:
+        block(1, lambda piece: None)
+        block(0, lambda piece: long_step(3, 1) if piece == 0 else None)
+        short_step(2, 1)
+        wide_first()
+        long_step(3, 0)
+        input_grad(1)
+        wide_second()
+        long_step(2, 1)
+        input_grad(0)
+        short_step(2, 0)
+        short_step(1, 1)
+        wide_others()
+        long_step(2, 0)
+        wide_step(long, 3)
+        wide_step(short, 2)
+        long_step(1, 1)
+        short_step(1, 0)
+        long_step(1, 0)
+        wide_step(long, 2)
+        wide_step(short, 1)
+    else:
+        block(1, lambda piece: None)
+        block(0, lambda piece: None)
+        input_grad(1)
+        input_grad(0)
+        wide_first()
+        wide_second()
+        wide_others()
+        for d in range(far - 1, 0, -1):
+            for b in (1, 0):
+                long_step(d, b)
+                short_step(d - 1, b)
+            if d > 1:
+                wide_step(long, d)
+                if d > 2:
+                    wide_step(short, d - 1)
 
     def reduced(b, h):
         return (
@@ -315,6 +353,8 @@
     out1[NH] = reduced(0, 1 - half).astype(BF16)
     late_copy(NH).start()
 
+    wide_step(long, 1)
+
     def late_wait(slot):
         pltpu.make_async_remote_copy(
             src_ref=out1.at[0],
@@ -327,7 +367,6 @@
 
     for slot in range(3):
         late_wait(slot)
-    scale = 1.0 / float(total_rows) ** 0.5
     for direction in range(2):
         for g in range(2):
             wide_message(direction, g, 1).wait_recv()
@@ -351,15 +390,16 @@
             + wide_ring[0, g, 0].astype(F32)
             + wide_ring[1, g, 0].astype(F32)
         )
-    totals = (total_of(0, ff), total_of(ff, 2 * ff), jnp.concatenate(pieces, axis=0))
-    for total, mom, new in zip(totals, (mg_ref, mu_ref, md_ref), (ng_ref, nu_ref, nd_ref)):
-        new[0] = 0.9 * mom[0] + total.T * scale
+    total_ref[0:ff, :] = total_of(0, ff)
+    total_ref[ff : 2 * ff, :] = total_of(ff, 2 * ff)
+    total_ref[2 * ff : three, :] = jnp.concatenate(pieces, axis=0)
 
     for h in range(NH):
         late_copy(h).wait_send()
     late_copy(NH).wait_send()
     for n in range(NH + 1):
-        wide_copy(n).wait_send()
+        for piece in range(pairs):
+            wide_copy(n, piece).wait_send()
     for d in range(1, far + 1):
         for direction, g in long + (short if d < far else ()):
             wide_message(direction, g, d).wait_send()
@@ -385,6 +425,44 @@
     @pl.when(sec == ns - 1)
     def _():
         zero_copy(1).wait()
+
+
+def finish_kernel(
+    scale, gin, total_hbm, mg, mu, md, grad_in, ng, nu, nd,
+    buf, total, mom, new, in_sem, out_sem, total_sem, mom_sem, new_sem,
+):
+    count, rows, _ = buf.shape
+    per = gin.shape[2] // rows
+    ff = total.shape[0] // 3
+
+    def move(n, out):
+        b, row = n // per, n % per * rows
+        if out:
+            return pltpu.make_async_copy(
+                buf.at[n], grad_in.at[0, b, pl.ds(row, rows)], out_sem.at[n]
+            )
+        return pltpu.make_async_copy(gin.at[0, b, pl.ds(row, rows)], buf.at[n], in_sem.at[n])
+
+    moms = [pltpu.make_async_copy(m.at[0], mom.at[n], mom_sem.at[n]) for n, m in enumerate((mg, mu, md))]
+    news = [pltpu.make_async_copy(new.at[n], m.at[0], new_sem.at[n]) for n, m in enumerate((ng, nu, nd))]
+    totals = pltpu.make_async_copy(total_hbm, total, total_sem)
+    totals.start()
+    for copy in moms:
+        copy.start()
+    for n in range(count):
+        move(n, False).start()
+    totals.wait()
+    for n in range(3):
+        moms[n].wait()
+        new[n] = 0.9 * mom[n] + total[n * ff : (n + 1) * ff, :].T * scale
+        news[n].start()
+    for n in range(count):
+        move(n, False).wait()
+        move(n, True).start()
+    for copy in news:
+        copy.wait()
+    for n in range(count):
+        move(n, True).wait()
 
 
 def body(inputs, cotangent, w_gate, w_up, w_down, mom_gate, mom_up, mom_down):
@@ -399,16 +477,14 @@
     anywhere = pl.BlockSpec(memory_space=pl.ANY)
     vmem = pl.BlockSpec(memory_space=pltpu.VMEM)
     dma = pltpu.SemaphoreType.DMA
-    return pl.pallas_call(
+    gin, total = pl.pallas_call(
         functools.partial(kernel, ns, nz, tok, dim, ff, cross),
         out_shape=(
             jax.ShapeDtypeStruct(inputs.shape, BF16),
-            jax.ShapeDtypeStruct(mom_gate.shape, F32),
-            jax.ShapeDtypeStruct(mom_up.shape, F32),
-            jax.ShapeDtypeStruct(mom_down.shape, F32),
+            jax.ShapeDtypeStruct((3 * ff, width), F32),
         ),
-        in_specs=[anywhere] * 5 + [vmem] * 3,
-        out_specs=(anywhere, vmem, vmem, vmem),
+        in_specs=[anywhere] * 5,
+        out_specs=(anywhere, vmem),
         scratch_shapes=[
             pltpu.VMEM((2, tok, dim), BF16),
             pltpu.VMEM((2, tok, dim), BF16),
@@ -434,8 +510,8 @@
             dma,
             dma((NH + 1,)),
             dma((NH + 1,)),
-            dma((NH + 1,)),
-            dma((NH + 1,)),
+            dma((NH + 1, nz // 2)),
+            dma((NH + 1, nz // 2)),
             dma((2, 2, far)),
             dma((2, 2, far)),
         ],
@@ -443,7 +519,32 @@
             collective_id=0, has_side_effects=True, vmem_limit_bytes=56 * 2**20
         ),
         name="relay_step",
-    )(inputs, cotangent, w_gate, w_up, w_down, mom_gate, mom_up, mom_down)
+    )(inputs, cotangent, w_gate, w_up, w_down)
+    count = 4
+    return pl.pallas_call(
+        functools.partial(finish_kernel, 1.0 / float(tok * NH * nz) ** 0.5),
+        out_shape=(
+            jax.ShapeDtypeStruct(inputs.shape, BF16),
+            jax.ShapeDtypeStruct(mom_gate.shape, F32),
+            jax.ShapeDtypeStruct(mom_up.shape, F32),
+            jax.ShapeDtypeStruct(mom_down.shape, F32),
+        ),
+        in_specs=[anywhere] * 5,
+        out_specs=(anywhere,) * 4,
+        scratch_shapes=[
+            pltpu.VMEM((count, 2 * tok // count, dim), BF16),
+            pltpu.VMEM((3 * ff, width), F32),
+            pltpu.VMEM((3, width, ff), F32),
+            pltpu.VMEM((3, width, ff), F32),
+            dma((count,)),
+            dma((count,)),
+            dma,
+            dma((3,)),
+            dma((3,)),
+        ],
+        compiler_params=pltpu.CompilerParams(vmem_limit_bytes=56 * 2**20),
+        name="relay_finish",
+    )(gin, total, mom_gate, mom_up, mom_down)
 
 
 def solution(mesh):

time: 78.8 us -> 72.6 us (0.921)
  the two profiles are of different devices: /device:TPU:1 before, /device:TPU:26 now
where the time goes in v3:
time: 72.6 us; the launch traced here: 72.5 us
  Pallas kernels  71.9 us (99%)
    pallas_call x1, Pallas kernels, body(): pl.pallas_call(functools.partial(kernel, ns, nz, tok, dim, ff, cross), ou...  68.5 us
    pallas_call x1, Pallas kernels, body(): pl.pallas_call(functools.partial(finish_kernel, 1.0 / float(tok * NH * nz...  3.35 us

profile of v3, /device:TPU:26, one launch (start us, length us, event | category | flops | bytes accessed | tf_op | source)
XLA Modules:
  0.0 72.5 jit_solution(7806409010148125959)
XLA Ops:
  0.6 68.5 %relay_step.1 = (bf16[1,2,256,2048]{3,2,1,0:T(8,128)(2,1)}, f32[768,128]{1,0:T(8,128)}) custom-call(bf16[1,2,256,2048]{3,2,1,0:T(8,128)(2,1)} %x_hbm.1, bf16[1,2,256,2048]{3,2,1,0:T(8,128)(2,1)} %y_hbm.1, bf16[1,2,2048,256]{3,2,1,0:T(8,128)(2,1)} %wg_hbm.1, bf16[1,2,2048,256]{3,2,1,0:T(8,128)(2,1)} %wu_hbm.1, bf16[1,2,256,2048]{3,2,1,0:T(8,128)(2,1)} %wd_hbm.1), custom_call_target="tpu_custom_call" | custom-call | tf_op jit(solution)/shard_map/relay_step/pallas_call | solution.py:480
  69.2 3.3 %relay_finish.1 = (bf16[1,2,256,2048]{3,2,1,0:T(8,128)(2,1)}, f32[1,128,256]{2,1,0:T(8,128)}, f32[1,128,256]{2,1,0:T(8,128)}, f32[1,128,256]{2,1,0:T(8,128)}) custom-call(bf16[1,2,256,2048]{3,2,1,0:T(8,128)(2,1)} %get-tuple-element.6.gin, f32[768,128]{1,0:T(8,128)} %get-tuple-element.7.total_hbm, f32[1,128,256]{2,1,0:T(8,128)} %mg.1, f32[1,128,256]{2,1,0:T(8,128)} %mu.1, ...), custom_call_target="tpu_custom_call" | custom-call | tf_op jit(solution)/shard_map/relay_finish/pallas_call | solution.py:524

commit v4 on v3

--- a/solution.py
+++ b/solution.py
@@ -9,7 +9,7 @@
 
 MESH = pl.DeviceIdType.MESH
 NH = 2
-CROSS = 0.25
+CROSS = 0.2917
 BF16 = jnp.bfloat16
 F32 = jnp.float32
 
@@ -216,12 +216,16 @@
         @pl.when(sends)
         def _():
             lax.fori_loop(0, dim // cut, dx_chunk, 0)
-            dx_copy(b).start()
 
         @pl.when(jnp.logical_not(sends))
         def _():
             dxb[b] = jnp.zeros((tok, dim), BF16)
             zero_copy(b).start()
+
+    def send_dx(b):
+        @pl.when(sec > 0 if b == 0 else sec < ns - 1)
+        def _():
+            dx_copy(b).start()
 
     def ring_step(lanes, d, b):
         for direction, h in lanes:
@@ -293,7 +297,10 @@
         input_grad(0)
         short_step(2, 0)
         short_step(1, 1)
+
         wide_others()
+        send_dx(1)
+        send_dx(0)
         long_step(2, 0)
         wide_step(long, 3)
         wide_step(short, 2)
@@ -307,6 +314,8 @@
         block(0, lambda piece: None)
         input_grad(1)
         input_grad(0)
+        send_dx(1)
+        send_dx(0)
         wide_first()
         wide_second()
         wide_others()

time: 72.6 us -> 69.9 us (0.963)
  the two profiles are of different devices: /device:TPU:26 before, /device:TPU:1 now
where the time goes in v4:
time: 69.9 us; the launch traced here: 69.7 us
  Pallas kernels  69.1 us (99%)
    pallas_call x1, Pallas kernels, body(): pl.pallas_call(functools.partial(kernel, ns, nz, tok, dim, ff, cross), ou...  65.8 us
    pallas_call x1, Pallas kernels, body(): pl.pallas_call(functools.partial(finish_kernel, 1.0 / float(tok * NH * nz...  3.35 us

profile of v4, /device:TPU:1, one launch (start us, length us, event | category | flops | bytes accessed | tf_op | source)
XLA Modules:
  0.0 69.7 jit_solution(13716083636946752758)
XLA Ops:
  0.6 65.8 %relay_step.1 = (bf16[1,2,256,2048]{3,2,1,0:T(8,128)(2,1)}, f32[768,128]{1,0:T(8,128)}) custom-call(bf16[1,2,256,2048]{3,2,1,0:T(8,128)(2,1)} %x_hbm.1, bf16[1,2,256,2048]{3,2,1,0:T(8,128)(2,1)} %y_hbm.1, bf16[1,2,2048,256]{3,2,1,0:T(8,128)(2,1)} %wg_hbm.1, bf16[1,2,2048,256]{3,2,1,0:T(8,128)(2,1)} %wu_hbm.1, bf16[1,2,256,2048]{3,2,1,0:T(8,128)(2,1)} %wd_hbm.1), custom_call_target="tpu_custom_call" | custom-call | tf_op jit(solution)/shard_map/relay_step/pallas_call | solution.py:489
  66.4 3.3 %relay_finish.1 = (bf16[1,2,256,2048]{3,2,1,0:T(8,128)(2,1)}, f32[1,128,256]{2,1,0:T(8,128)}, f32[1,128,256]{2,1,0:T(8,128)}, f32[1,128,256]{2,1,0:T(8,128)}) custom-call(bf16[1,2,256,2048]{3,2,1,0:T(8,128)(2,1)} %get-tuple-element.6.gin, f32[768,128]{1,0:T(8,128)} %get-tuple-element.7.total_hbm, f32[1,128,256]{2,1,0:T(8,128)} %mg.1, f32[1,128,256]{2,1,0:T(8,128)} %mu.1, ...), custom_call_target="tpu_custom_call" | custom-call | tf_op jit(solution)/shard_map/relay_finish/pallas_call | solution.py:533

commit v5 on v4

--- a/solution.py
+++ b/solution.py
@@ -40,17 +40,16 @@
     def device(s, h, zz):
         return (s, h * nz + zz)
 
-    loads = []
-    for b in (1, 0):
+    def start_loads(b):
         for n, (src, dst) in enumerate(
             ((x_hbm, xb), (wg_hbm, wgb), (wu_hbm, wub), (y_hbm, yb), (wd_hbm, wdb))
         ):
-            copy = pltpu.make_async_copy(src.at[0, b], dst.at[b], in_sem.at[b, n])
-            copy.start()
-            loads.append(copy)
+            load(b, n, src, dst).start()
 
     def load(b, n, src, dst):
         return pltpu.make_async_copy(src.at[0, b], dst.at[b], in_sem.at[b, n])
+
+    start_loads(1)
 
     barrier = pltpu.get_barrier_semaphore()
     neighbours = [
@@ -69,6 +68,8 @@
         b = 1 - i
         load(b, 0, x_hbm, xb).wait()
         load(b, 1, wg_hbm, wgb).wait()
+        if b == 1:
+            start_loads(0)
         pre[0] = jnp.dot(xb[b], wgb[b], preferred_element_type=F32)
         load(b, 2, wu_hbm, wub).wait()
         pre[1] = jnp.dot(xb[b], wub[b], preferred_element_type=F32)
@@ -296,19 +297,18 @@
         long_step(2, 1)
         input_grad(0)
         short_step(2, 0)
-        short_step(1, 1)
-
         wide_others()
         send_dx(1)
         send_dx(0)
+        short_step(1, 1)
         long_step(2, 0)
         wide_step(long, 3)
         wide_step(short, 2)
         long_step(1, 1)
         short_step(1, 0)
-        long_step(1, 0)
         wide_step(long, 2)
         wide_step(short, 1)
+        long_step(1, 0)
     else:
         block(1, lambda piece: None)
         block(0, lambda piece: None)
@@ -455,19 +455,19 @@
     moms = [pltpu.make_async_copy(m.at[0], mom.at[n], mom_sem.at[n]) for n, m in enumerate((mg, mu, md))]
     news = [pltpu.make_async_copy(new.at[n], m.at[0], new_sem.at[n]) for n, m in enumerate((ng, nu, nd))]
     totals = pltpu.make_async_copy(total_hbm, total, total_sem)
+    for n in range(count):
+        move(n, False).start()
     totals.start()
     for copy in moms:
         copy.start()
     for n in range(count):
-        move(n, False).start()
+        move(n, False).wait()
+        move(n, True).start()
     totals.wait()
     for n in range(3):
         moms[n].wait()
         new[n] = 0.9 * mom[n] + total[n * ff : (n + 1) * ff, :].T * scale
         news[n].start()
-    for n in range(count):
-        move(n, False).wait()
-        move(n, True).start()
     for copy in news:
         copy.wait()
     for n in range(count):

time: 69.9 us -> 68.7 us (0.983)
  Pallas kernels: 69.1 us -> 68 us
where the time goes in v5:
time: 68.7 us; the launch traced here: 68.6 us
  Pallas kernels  68 us (99%)
    pallas_call x1, Pallas kernels, body(): pl.pallas_call(functools.partial(kernel, ns, nz, tok, dim, ff, cross), ou...  65.1 us
    pallas_call x1, Pallas kernels, body(): pl.pallas_call(functools.partial(finish_kernel, 1.0 / float(tok * NH * nz...  2.81 us

profile of v5, /device:TPU:1, one launch (start us, length us, event | category | flops | bytes accessed | tf_op | source)
XLA Modules:
  0.0 68.6 jit_solution(8322408630351808631)
XLA Ops:
  0.6 65.1 %relay_step.1 = (bf16[1,2,256,2048]{3,2,1,0:T(8,128)(2,1)}, f32[768,128]{1,0:T(8,128)}) custom-call(bf16[1,2,256,2048]{3,2,1,0:T(8,128)(2,1)} %x_hbm.1, bf16[1,2,256,2048]{3,2,1,0:T(8,128)(2,1)} %y_hbm.1, bf16[1,2,2048,256]{3,2,1,0:T(8,128)(2,1)} %wg_hbm.1, bf16[1,2,2048,256]{3,2,1,0:T(8,128)(2,1)} %wu_hbm.1, bf16[1,2,256,2048]{3,2,1,0:T(8,128)(2,1)} %wd_hbm.1), custom_call_target="tpu_custom_call" | custom-call | tf_op jit(solution)/shard_map/relay_step/pallas_call | solution.py:489
  65.8 2.8 %relay_finish.1 = (bf16[1,2,256,2048]{3,2,1,0:T(8,128)(2,1)}, f32[1,128,256]{2,1,0:T(8,128)}, f32[1,128,256]{2,1,0:T(8,128)}, f32[1,128,256]{2,1,0:T(8,128)}) custom-call(bf16[1,2,256,2048]{3,2,1,0:T(8,128)(2,1)} %get-tuple-element.6.gin, f32[768,128]{1,0:T(8,128)} %get-tuple-element.7.total_hbm, f32[1,128,256]{2,1,0:T(8,128)} %mg.1, f32[1,128,256]{2,1,0:T(8,128)} %mu.1, ...), custom_call_target="tpu_custom_call" | custom-call | tf_op jit(solution)/shard_map/relay_finish/pallas_call | solution.py:533

commit v6 on v5

--- a/solution.py
+++ b/solution.py
@@ -292,8 +292,8 @@
         short_step(2, 1)
         wide_first()
         long_step(3, 0)
+        wide_second()
         input_grad(1)
-        wide_second()
         long_step(2, 1)
         input_grad(0)
         short_step(2, 0)

time: 68.7 us -> 68.7 us (level)
  no operation moved by 1% of the time
where the time goes in v6:
time: 68.7 us; the launch traced here: 68.6 us
  Pallas kernels  68 us (99%)
    pallas_call x1, Pallas kernels, body(): pl.pallas_call(functools.partial(kernel, ns, nz, tok, dim, ff, cross), ou...  65.1 us
    pallas_call x1, Pallas kernels, body(): pl.pallas_call(functools.partial(finish_kernel, 1.0 / float(tok * NH * nz...  2.81 us

profile of v6, /device:TPU:1, one launch (start us, length us, event | category | flops | bytes accessed | tf_op | source)
XLA Modules:
  0.0 68.6 jit_solution(8431922292405374403)
XLA Ops:
  0.6 65.1 %relay_step.1 = (bf16[1,2,256,2048]{3,2,1,0:T(8,128)(2,1)}, f32[768,128]{1,0:T(8,128)}) custom-call(bf16[1,2,256,2048]{3,2,1,0:T(8,128)(2,1)} %x_hbm.1, bf16[1,2,256,2048]{3,2,1,0:T(8,128)(2,1)} %y_hbm.1, bf16[1,2,2048,256]{3,2,1,0:T(8,128)(2,1)} %wg_hbm.1, bf16[1,2,2048,256]{3,2,1,0:T(8,128)(2,1)} %wu_hbm.1, bf16[1,2,256,2048]{3,2,1,0:T(8,128)(2,1)} %wd_hbm.1), custom_call_target="tpu_custom_call" | custom-call | tf_op jit(solution)/shard_map/relay_step/pallas_call | solution.py:489
  65.8 2.8 %relay_finish.1 = (bf16[1,2,256,2048]{3,2,1,0:T(8,128)(2,1)}, f32[1,128,256]{2,1,0:T(8,128)}, f32[1,128,256]{2,1,0:T(8,128)}, f32[1,128,256]{2,1,0:T(8,128)}) custom-call(bf16[1,2,256,2048]{3,2,1,0:T(8,128)(2,1)} %get-tuple-element.6.gin, f32[768,128]{1,0:T(8,128)} %get-tuple-element.7.total_hbm, f32[1,128,256]{2,1,0:T(8,128)} %mg.1, f32[1,128,256]{2,1,0:T(8,128)} %mu.1, ...), custom_call_target="tpu_custom_call" | custom-call | tf_op jit(solution)/shard_map/relay_finish/pallas_call | solution.py:533
